TPU v7x, 32 devices: a whole 2x2x4 slice. The times are simulated.
32 devices in a mesh: stream: 2 (over x), dp: 16 (over z, y, core).
Axes of the slice: x: 2, y: 2, z: 4, core: 2. Of those that a mesh axis runs over, the one named last changes fastest.
Arguments:
- tokens: bfloat16 [2, 16, 512, 768], P('stream', 'dp'), may hold values from -6 to 6
- boxes: int32 [2, 16, 2, 512], P('stream', 'dp'), may hold values from 0 to 1023
- rel_one: int32 [2, 16, 512, 512], P('stream', 'dp'), may hold values from 0 to 31
- rel_two: int32 [2, 16, 512, 512], P('stream', 'dp'), may hold values from 0 to 63
- vis_count: int32 [16], P('dp'), may hold values from 256 to 512, as said below
- spatial_tables: bfloat16 [2, 1024, 768], replicated, may hold values from -4.1875 to 4.1875
- proj_weights: bfloat16 [2, 2, 5, 768, 768], P('stream'), may hold values from -0.21875 to 0.21875
- out_weights: bfloat16 [2, 2, 768, 768], P('stream'), may hold values from -1.25 to 1.25
- ffn_in: bfloat16 [2, 2, 768, 3072], P('stream'), may hold values from -0.21875 to 0.21875
- ffn_out: bfloat16 [2, 2, 3072, 768], P('stream'), may hold values from -0.109375 to 0.109375
- norm_gains: float32 [2, 2, 2, 768], P('stream'), may hold values from 0.5 to 1.5
- norm_shifts: float32 [2, 2, 2, 768], P('stream'), may hold values from -1.8 to 1.8
- bias_tables: bfloat16 [2, 2, 12, 96], P('stream'), may hold values from -6 to 6
- cotangent: bfloat16 [2, 16, 512, 768], P('stream', 'dp'), may hold values from -6 to 6
Outputs:
- output: bfloat16 [2, 16, 512, 768], P('stream', 'dp')
- grad_tokens: float32 [2, 16, 512, 768], P('stream', 'dp')
- grad_spatial: float32 [2, 1024, 768], replicated
- grad_proj: float32 [2, 2, 5, 768, 768], P('stream', None, None, 'dp')
- grad_out: float32 [2, 2, 768, 768], P('stream', None, 'dp')
- grad_ffn_in: float32 [2, 2, 768, 3072], P('stream', None, 'dp')
- grad_ffn_out: float32 [2, 2, 3072, 768], P('stream', None, 'dp')
- grad_gains: float32 [2, 2, 2, 768], P('stream', None, None, 'dp')
- grad_shifts: float32 [2, 2, 2, 768], P('stream', None, None, 'dp')
- grad_tables: float32 [2, 2, 12, 96], P('stream')
Inputs may be any that keep to these rules, and one draw needn't show every extreme that they name: `vis_count`: each page has 256 or 512 visual tokens; the first page always has 512, the second 512 // 2.
All inputs are finite; a program needn't handle non-finite values.
Results may differ from a plain program's by a relative error of at most 0.035.
The roundings to bfloat16 on the way count: a program that leaves them out, or rounds other values in their place, can miss the bound.
Values sent between devices are 32-bit elements; how exact they have to be, the bound alone decides.
No kernel may reach another device: no remote copies, remote signals or barrier semaphores. Data moves between devices by JAX's collectives and lax.ppermute only.
A program may use at most 384 MiB of HBM per device.

v0:
```python
from functools import partial
import jax
import jax.numpy as jnp
from jax import lax
from jax.sharding import PartitionSpec as P

D = 768
HEADS = 12
HD = 64
NB1 = 32
NB2 = 64
LAYERS = 2
NEG_FILL = -1e30


def layer_norm(values, gain_vec, shift_vec):
    center = values - jnp.mean(values, axis=-1, keepdims=True)
    spread = jnp.mean(center * center, axis=-1, keepdims=True)
    return center * lax.rsqrt(spread + 1e-05) * gain_vec + shift_vec


def mixed_dot(formula, left, right):
    return jnp.einsum(formula, left, right, preferred_element_type=jnp.float32)


def bucket_lookup(rel_first, rel_second, bucket_table):
    first_hot = (rel_first[:, :, None] == jnp.arange(NB1, dtype=jnp.int32)[None, None, :]).astype(
        jnp.bfloat16
    )
    second_hot = (rel_second[:, :, None] == jnp.arange(NB2, dtype=jnp.int32)[None, None, :]).astype(
        jnp.bfloat16
    )
    bucket_bias = mixed_dot("qkb,hb->hqk", first_hot, bucket_table[:, :NB1]) + mixed_dot(
        "qkb,hb->hqk", second_hot, bucket_table[:, NB1:]
    )
    return (bucket_bias, first_hot, second_hot)


def page_scores(query_cat, key_cat, rel_first, rel_second, key_valid, bucket_table):
    bucket_bias, first_hot, second_hot = bucket_lookup(rel_first, rel_second, bucket_table)
    scores = mixed_dot("qhd,khd->hqk", query_cat, key_cat) * HD ** (-0.5) + bucket_bias
    scores = jnp.where(key_valid[None, None, :], scores, NEG_FILL)
    return (scores, first_hot, second_hot)


def page_forward(inputs, bucket_table):
    query_cat, key_cat, value_heads, rel_first, rel_second, key_valid = inputs
    scores, first_hot, second_hot = page_scores(
        query_cat, key_cat, rel_first, rel_second, key_valid, bucket_table
    )
    row_top = jnp.max(scores, axis=-1, keepdims=True)
    exp_scores = jnp.exp(scores - row_top)
    row_total = jnp.sum(exp_scores, axis=-1, keepdims=True)
    prob_low = (exp_scores / row_total).astype(jnp.bfloat16)
    context = mixed_dot("hqk,khd->qhd", prob_low, value_heads).astype(jnp.bfloat16)
    return (context, (row_top + jnp.log(row_total))[:, :, 0])


def page_backward(inputs, bucket_table):
    query_cat, key_cat, value_heads, rel_first, rel_second, key_valid, log_total, context_grad = (
        inputs
    )
    scores, first_hot, second_hot = page_scores(
        query_cat, key_cat, rel_first, rel_second, key_valid, bucket_table
    )
    prob_full = jnp.exp(scores - log_total[:, :, None])
    prob_low = prob_full.astype(jnp.bfloat16)
    prob_grad = mixed_dot("qhd,khd->hqk", context_grad, value_heads)
    score_grad = (
        prob_full * (prob_grad - jnp.sum(prob_full * prob_grad, axis=-1, keepdims=True))
    ).astype(jnp.bfloat16)
    score_scale = HD ** (-0.5)
    query_grad = (mixed_dot("hqk,khd->qhd", score_grad, key_cat) * score_scale).astype(jnp.bfloat16)
    key_grad = (mixed_dot("hqk,qhd->khd", score_grad, query_cat) * score_scale).astype(jnp.bfloat16)
    value_grad = mixed_dot("hqk,qhd->khd", prob_low, context_grad).astype(jnp.bfloat16)
    table_grad = jnp.concatenate(
        [
            mixed_dot("hqk,qkb->hb", score_grad, first_hot),
            mixed_dot("hqk,qkb->hb", score_grad, second_hot),
        ],
        axis=1,
    )
    return (query_grad, key_grad, value_grad, table_grad)


def head_layout(token_proj, spatial_proj, page_count):
    length = token_proj.shape[1] // page_count

    def to_heads(values):
        return values.reshape(page_count, length, HEADS, HD)

    query_cat = jnp.concatenate([to_heads(token_proj[0]), to_heads(spatial_proj[0])], axis=-1)
    key_cat = jnp.concatenate([to_heads(token_proj[1]), to_heads(spatial_proj[1])], axis=-1)
    return (query_cat, key_cat, to_heads(token_proj[2]))


def layer_forward(hidden_in, spatial, weights, layout):
    projections, out_proj, w_in, w_out, gains, shifts, bucket_table = weights
    rel_first, rel_second, key_valid, rowmask = layout
    page_count = rel_first.shape[0]
    row_count = hidden_in.shape[0]
    rounded = hidden_in.astype(jnp.bfloat16)
    token_proj = mixed_dot("rd,jde->jre", rounded, projections[:3]).astype(jnp.bfloat16)
    spatial_proj = mixed_dot("rd,jde->jre", spatial, projections[3:]).astype(jnp.bfloat16)
    query_cat, key_cat, value_heads = head_layout(token_proj, spatial_proj, page_count)
    context, log_total = lax.map(
        partial(page_forward, bucket_table=bucket_table),
        (query_cat, key_cat, value_heads, rel_first, rel_second, key_valid),
    )
    context = context.reshape(row_count, D)
    attn_out = jnp.dot(context, out_proj, preferred_element_type=jnp.float32) * rowmask
    mixed = lax.psum(attn_out, "stream")
    pre_attn = hidden_in + mixed
    normed = layer_norm(pre_attn, gains[0], shifts[0])
    normed_low = normed.astype(jnp.bfloat16)
    inner_pre = jnp.dot(normed_low, w_in, preferred_element_type=jnp.float32)
    activated = jax.nn.gelu(inner_pre, approximate=False).astype(jnp.bfloat16)
    branch = jnp.dot(activated, w_out, preferred_element_type=jnp.float32)
    result = layer_norm(normed + branch, gains[1], shifts[1])
    kept_state = (
        rounded,
        token_proj,
        spatial_proj,
        context,
        log_total,
        pre_attn,
        normed,
        normed_low,
        inner_pre,
        activated,
        branch,
    )
    return (result, kept_state)


def gelu_exact(values):
    return jax.nn.gelu(values, approximate=False)


def layer_backward(result_grad, spatial, weights, layout, kept_state):
    projections, out_proj, w_in, w_out, gains, shifts, bucket_table = weights
    rel_first, rel_second, key_valid, rowmask = layout
    (
        rounded,
        token_proj,
        spatial_proj,
        context,
        log_total,
        pre_attn,
        normed,
        normed_low,
        inner_pre,
        activated,
        branch,
    ) = kept_state
    page_count = rel_first.shape[0]
    row_count = rounded.shape[0]
    length = row_count // page_count
    unused, norm_pull = jax.vjp(layer_norm, normed + branch, gains[1], shifts[1])
    sum_grad, gain_two, shift_two = norm_pull(result_grad)
    branch_low = sum_grad.astype(jnp.bfloat16)
    w_out_grad = mixed_dot("rf,rd->fd", activated, branch_low)
    act_grad = mixed_dot("rd,fd->rf", branch_low, w_out)
    unused, gelu_pull = jax.vjp(gelu_exact, inner_pre)
    inner_low = gelu_pull(act_grad)[0].astype(jnp.bfloat16)
    w_in_grad = mixed_dot("rd,rf->df", normed_low, inner_low)
    normed_grad = sum_grad + mixed_dot("rf,df->rd", inner_low, w_in)
    unused, first_pull = jax.vjp(layer_norm, pre_attn, gains[0], shifts[0])
    pre_grad, gain_one, shift_one = first_pull(normed_grad)
    mixed_grad = lax.psum(pre_grad, "stream")
    attn_low = (mixed_grad * rowmask).astype(jnp.bfloat16)
    out_grad = mixed_dot("rd,re->de", context, attn_low)
    context_grad = mixed_dot("re,de->rd", attn_low, out_proj).astype(jnp.bfloat16)
    query_cat, key_cat, value_heads = head_layout(token_proj, spatial_proj, page_count)
    query_grad, key_grad, value_grad, table_grads = lax.map(
        partial(page_backward, bucket_table=bucket_table),
        (
            query_cat,
            key_cat,
            value_heads,
            rel_first,
            rel_second,
            key_valid,
            log_total,
            context_grad.reshape(page_count, length, HEADS, HD),
        ),
    )
    token_grads = jnp.stack(
        [
            query_grad[..., :HD].reshape(row_count, D),
            key_grad[..., :HD].reshape(row_count, D),
            value_grad.reshape(row_count, D),
        ]
    )
    spatial_grads = jnp.stack(
        [query_grad[..., HD:].reshape(row_count, D), key_grad[..., HD:].reshape(row_count, D)]
    )
    proj_grad = jnp.concatenate(
        [
            mixed_dot("rd,jre->jde", rounded, token_grads),
            mixed_dot("rd,jre->jde", spatial, spatial_grads),
        ],
        axis=0,
    )
    input_grad = pre_grad + mixed_dot("jre,jde->rd", token_grads, projections[:3])
    spatial_part = mixed_dot("jre,jde->rd", spatial_grads, projections[3:])
    weight_grads = (
        proj_grad,
        out_grad,
        w_in_grad,
        w_out_grad,
        jnp.stack([gain_one, gain_two]),
        jnp.stack([shift_one, shift_two]),
    )
    return (input_grad, spatial_part, weight_grads, jnp.sum(table_grads, axis=0))


def local(
    tokens,
    boxes,
    rel_one,
    rel_two,
    vis_count,
    spatial_tables,
    proj_weights,
    out_weights,
    ffn_in,
    ffn_out,
    norm_gains,
    norm_shifts,
    bias_tables,
    cotangent,
):
    page_count = tokens.shape[1]
    length = tokens.shape[2]
    row_count = page_count * length
    stream_at = lax.axis_index("stream")
    counts = jnp.where(stream_at == 0, length, vis_count)
    key_valid = jnp.arange(length, dtype=jnp.int32)[None, :] < counts[:, None]
    rowmask = key_valid.reshape(row_count, 1).astype(jnp.float32)
    layout = (rel_one[0], rel_two[0], key_valid, rowmask)
    bin_ids = jnp.arange(spatial_tables.shape[1], dtype=jnp.int32)
    hot_x = (boxes[0, :, 0].reshape(row_count, 1) == bin_ids[None, :]).astype(jnp.bfloat16)
    hot_y = (boxes[0, :, 1].reshape(row_count, 1) == bin_ids[None, :]).astype(jnp.bfloat16)
    spatial = (
        jnp.dot(hot_x, spatial_tables[0], preferred_element_type=jnp.float32)
        + jnp.dot(hot_y, spatial_tables[1], preferred_element_type=jnp.float32)
    ).astype(jnp.bfloat16)

    def layer_weights(layer_at):
        return (
            proj_weights[0, layer_at],
            out_weights[0, layer_at],
            ffn_in[0, layer_at],
            ffn_out[0, layer_at],
            norm_gains[0, layer_at],
            norm_shifts[0, layer_at],
            bias_tables[0, layer_at],
        )

    hidden = tokens[0].reshape(row_count, D).astype(jnp.float32)
    inputs_kept = []
    states_kept = []
    for layer_at in range(LAYERS):
        inputs_kept.append(hidden)
        hidden, kept_state = layer_forward(hidden, spatial, layer_weights(layer_at), layout)
        states_kept.append(kept_state)
    output = (hidden * rowmask).astype(jnp.bfloat16).reshape(1, page_count, length, D)
    result_grad = cotangent[0].reshape(row_count, D).astype(jnp.float32) * rowmask
    spatial_grad = jnp.zeros((row_count, D), jnp.float32)
    layer_grads = []
    table_grads = []
    for layer_at in reversed(range(LAYERS)):
        kept_state = states_kept[layer_at]
        result_grad, spatial_part, weight_grads, table_part = layer_backward(
            result_grad, spatial, layer_weights(layer_at), layout, kept_state
        )
        spatial_grad = spatial_grad + spatial_part
        layer_grads.insert(0, weight_grads)
        table_grads.insert(0, table_part)
    stacked = tuple((jnp.stack(members) for members in zip(*layer_grads)))
    stacked = (
        lax.psum_scatter(stacked[0], "dp", scatter_dimension=2, tiled=True),
        lax.psum_scatter(stacked[1], "dp", scatter_dimension=1, tiled=True),
        lax.psum_scatter(stacked[2], "dp", scatter_dimension=1, tiled=True),
        lax.psum_scatter(stacked[3], "dp", scatter_dimension=1, tiled=True),
        lax.psum_scatter(stacked[4], "dp", scatter_dimension=2, tiled=True),
        lax.psum_scatter(stacked[5], "dp", scatter_dimension=2, tiled=True),
    )
    spatial_low = spatial_grad.astype(jnp.bfloat16)
    table_x = mixed_dot("rb,rd->bd", hot_x, spatial_low)
    table_y = mixed_dot("rb,rd->bd", hot_y, spatial_low)
    own_slot = (jnp.arange(2, dtype=jnp.int32) == stream_at).astype(jnp.float32)
    bucket_all = own_slot[:, None, None, None] * jnp.stack(table_grads)[None]
    shared, buckets = lax.psum((jnp.stack([table_x, table_y]), bucket_all), ("stream", "dp"))
    bucket_own = lax.dynamic_slice_in_dim(buckets, stream_at, 1, 0)
    return (
        output,
        result_grad.reshape(1, page_count, length, D),
        shared,
        stacked[0][None],
        stacked[1][None],
        stacked[2][None],
        stacked[3][None],
        stacked[4][None],
        stacked[5][None],
        bucket_own,
    )


def solution(mesh):
    placed = (
        P("stream", "dp", None, None),
        P("stream", "dp", None, None),
        P("stream", "dp", None, None),
        P("stream", "dp", None, None),
        P("dp"),
        P(),
        P("stream", None, None, None, None),
        P("stream", None, None, None),
        P("stream", None, None, None),
        P("stream", None, None, None),
        P("stream", None, None, None),
        P("stream", None, None, None),
        P("stream", None, None, None),
        P("stream", "dp", None, None),
    )
    return jax.shard_map(
        local,
        mesh=mesh,
        in_specs=placed,
        out_specs=(
            P("stream", "dp", None, None),
            P("stream", "dp", None, None),
            P(),
            P("stream", None, None, "dp", None),
            P("stream", None, "dp", None),
            P("stream", None, "dp", None),
            P("stream", None, "dp", None),
            P("stream", None, None, "dp"),
            P("stream", None, None, "dp"),
            P("stream", None, None, None),
        ),
        check_vma=False,
    )
```

profile of v0, /device:TPU:0, one launch (start us, length us, event | category | flops | bytes accessed | tf_op | source)
XLA Modules:
  0.0 1694.1 jit_solution(16295816301324897043)
XLA Ops:
  15.2 14.9 fusion.3
  30.2 8.5 fusion.11
  60.7 31.0 %fusion.242 = (f32[12,512]{1,0:T(8,128)S(1)}, f32[12,512,512]{1,2,0:T(8,128)}) fusion(f32[512,512,12]{0,2,1:T(8,128)} %fusion.3, f32[512,512,12]{0,2,1:T(8,128)} %fusion.11, bf16[1,512,12,64]{3,1,2,0:T(8,128)(2,1)} %copy.153, bf16[1,512,12,64]{3,1,2,0:T(8,128)(2,1)} %copy.152, bf16[1,512,12,64]{3,1,2,0:T(8,128)(2,1)} %copy.150, ...), kind=kOutput, calls=%fused_computation.338 | convolution fusion | flops 827320320 | bytes 40919552 | tf_op jit(solution)/shard_map/while/body/eval_jaxpr/qhd,khd->hqk/dot_general | solution.py:23
  118.5 8.6 fusion.10
  127.1 14.4 fusion.2
  141.5 18.1 %all-reduce.8.cloned.1.call-done = f32[512,768]{1,0:T(8,128)} async-done(((f32[512,768]{1,0:T(8,128)}), f32[512,768]{1,0:T(8,128)}) %all-reduce.8.cloned.1.call-update) | async-done | bytes 1572880 | tf_op jit(solution)/shard_map/psum | solution.py:112
  162.6 20.2 %multiply_convert_fusion.3 = (bf16[512,3072]{1,0:T(8,128)(2,1)S(1)}, f32[512,3072]{1,0:T(8,128)}, f32[512,3072]{1,0:T(8,128)}) fusion(bf16[1,2,768,3072]{3,2,1,0:T(8,128)(2,1)} %param.22, f32[512,768]{1,0:T(8,128)S(1)} %get-tuple-element.219, f32[768]{0:T(1024)S(1)} %get-tuple-element.202, f32[768]{0:T(1024)S(1)} %get-tuple-element.265, ...), kind=kOutput, calls=%fused_computation.71 | convolution fusion | flops 2520121344 | bytes 22030336 | tf_op jit(solution)/shard_map/dot_general | solution.py:116
  201.6 30.3 %fusion.244 = (f32[12,512]{1,0:T(8,128)S(1)}, f32[12,512,512]{1,2,0:T(8,128)}) fusion(f32[512,512,12]{0,2,1:T(8,128)} %fusion.2, f32[512,512,12]{0,2,1:T(8,128)} %fusion.10, bf16[1,512,12,64]{3,1,2,0:T(8,128)(2,1)S(1)} %copy-done.12, bf16[1,512,12,64]{3,1,2,0:T(8,128)(2,1)} %copy.169, bf16[1,512,12,64]{3,1,2,0:T(8,128)(2,1)S(1)} %copy-done.13, ...), kind=kOutput, calls=%fused_computation.340 | convolution fusion | flops 827320320 | bytes 40919552 | tf_op jit(solution)/shard_map/while/body/eval_jaxpr/qhd,khd->hqk/dot_general | solution.py:23
  246.8 51.6 %all-reduce.10.cloned.1.call-done = f32[512,768]{1,0:T(8,128)} async-done(((f32[512,768]{1,0:T(8,128)}), f32[512,768]{1,0:T(8,128)}) %all-reduce.10.cloned.1.call-update) | async-done | bytes 1572880 | tf_op jit(solution)/shard_map/psum | solution.py:112
  301.3 20.1 %multiply_convert_fusion.2 = (bf16[512,3072]{1,0:T(8,128)(2,1)S(1)}, f32[512,3072]{1,0:T(8,128)}, f32[512,3072]{1,0:T(8,128)}) fusion(bf16[1,2,768,3072]{3,2,1,0:T(8,128)(2,1)} %param.22, f32[512,768]{1,0:T(8,128)S(1)} %get-tuple-element.215, f32[768]{0:T(1024)S(1)} %get-tuple-element.203, f32[768]{0:T(1024)S(1)} %get-tuple-element.264, ...), kind=kOutput, calls=%fused_computation.58 | convolution fusion | flops 2520121344 | bytes 22030336 | tf_op jit(solution)/shard_map/dot_general | solution.py:116
  327.1 8.8 add_convert_fusion.1
  344.8 51.5 %all-reduce.12.cloned.1.call-done = f32[512,768]{1,0:T(8,128)} async-done(((f32[512,768]{1,0:T(8,128)}), f32[512,768]{1,0:T(8,128)}) %all-reduce.12.cloned.1.call-update) | async-done | bytes 1572880 | tf_op jit(solution)/shard_map/psum | solution.py:170
  402.1 7.9 fusion.155
  410.0 9.4 multiply_reduce_fusion.1
  449.8 10.1 add_convert_fusion
  485.8 10.0 maximum_bitcast_fusion.1
  497.7 21.0 %all-reduce.14.cloned.1.call-done = f32[512,768]{1,0:T(8,128)} async-done(((f32[512,768]{1,0:T(8,128)}), f32[512,768]{1,0:T(8,128)}) %all-reduce.14.cloned.1.call-update) | async-done | bytes 1572880 | tf_op jit(solution)/shard_map/psum | solution.py:170
  521.6 7.7 fusion.158
  529.3 9.2 multiply_reduce_fusion
  576.5 10.1 maximum_bitcast_fusion
  586.6 16.6 pad_maximum_fusion
  603.2 35.0 %copy.204 = f32[2,5,768,768]{3,0,1,2:T(2,128)} copy(f32[2,5,768,768]{2,3,1,0:T(8,128)} %pad_maximum_fusion) | data formatting | bytes 47185920 | tf_op jit(solution)/shard_map/stack | solution.py:281
  693.0 10.1 fusion.177
  703.1 14.1 fusion.183
  720.3 10.6 fusion.174
  730.9 14.0 fusion.180
  745.1 40.8 %psum.47 = f32[2,2,12,96]{3,1,2,0:T(2,128)S(1)} all-reduce(f32[2,2,12,96]{3,1,2,0:T(2,128)S(1)} %broadcast_multiply_fusion), channel_id=1, replica_groups=mesh['stream'=2,'dp'=16] {'stream','dp'}, use_global_device_ids=true, to_apply=%region_41.42 | all-reduce | flops 4608 | bytes 36864 | tf_op jit(solution)/shard_map/psum | solution.py:295
  792.4 249.3 %all-reduce.18.cloned.1.call-done = f32[2,5,768,768]{3,0,1,2:T(2,128)} async-done(((f32[2,5,768,768]{3,0,1,2:T(2,128)}), f32[2,5,768,768]{3,0,1,2:T(2,128)}) %all-reduce.18.cloned.1.call-update) | async-done | bytes 23592976
  1044.9 159.0 %all-reduce.16.cloned.1.call-done = f32[2,1024,768]{2,1,0:T(8,128)} async-done(((f32[2,1024,768]{2,1,0:T(8,128)}), f32[2,1024,768]{2,1,0:T(8,128)}) %all-reduce.16.cloned.1.call-update) | async-done | bytes 6291472 | tf_op jit(solution)/shard_map/psum | solution.py:295
  1203.9 80.3 %reduce-scatter.10.cloned.1.call-done = f32[2,48,768]{2,1,0:T(8,128)} async-done(((f32[2,768,768]{2,1,0:T(8,128)}), f32[2,48,768]{2,1,0:T(8,128)}) %reduce-scatter.10.cloned.1.call-update) | async-done | bytes 294928 | tf_op jit(solution)/shard_map/reduce_scatter | solution.py:284
  1284.2 198.6 %reduce-scatter.12.cloned.1.call-done = f32[2,48,3072]{2,1,0:T(8,128)} async-done(((f32[2,768,3072]{2,1,0:T(8,128)}), f32[2,48,3072]{2,1,0:T(8,128)}) %reduce-scatter.12.cloned.1.call-update) | async-done | bytes 1179664 | tf_op jit(solution)/shard_map/reduce_scatter | solution.py:285
  1482.8 198.8 %reduce-scatter.14.cloned.1.call-done = f32[2,192,768]{2,1,0:T(8,128)} async-done(((f32[2,3072,768]{2,1,0:T(8,128)}), f32[2,192,768]{2,1,0:T(8,128)}) %reduce-scatter.14.cloned.1.call-update) | async-done | bytes 1179664 | tf_op jit(solution)/shard_map/reduce_scatter | solution.py:286
  (413 shorter events, 286.6 us)
Async XLA Ops:
  7.2 152.5 %all-reduce.8.cloned.1.call-start = ((), (), s32[]{:S(2)}) async-start(), calls=%async_computation.5 | async-start | bytes 3145728 | tf_op jit(solution)/shard_map/psum | solution.py:112
  12.9 85.5 %copy-start.25 = (bf16[1,512,768]{1,2,0:T(8,128)(2,1)}, bf16[1,512,768]{1,2,0:T(8,128)(2,1)S(1)}, u32[]{:S(2)}) copy-start(bf16[1,512,768]{1,2,0:T(8,128)(2,1)S(1)} %get-tuple-element.225) | copy-start | bytes 2359300
  13.3 113.9 %copy-start.6 = (s32[512,512]{0,1:T(8,128)}, s32[512,512]{0,1:T(8,128)S(1)}, u32[]{:S(2)}) copy-start(s32[512,512]{0,1:T(8,128)S(1)} %copy.157) | copy-start | bytes 3145732
  15.2 103.3 %copy-start.4 = (s32[512,512]{0,1:T(8,128)}, s32[512,512]{0,1:T(8,128)S(1)}, u32[]{:S(2)}) copy-start(s32[512,512]{0,1:T(8,128)S(1)} %copy.154) | copy-start | bytes 3145732
  105.3 193.1 %all-reduce.10.cloned.1.call-start = ((), (), s32[]{:S(2)}) async-start(), calls=%async_computation.6 | async-start | bytes 3145728 | tf_op jit(solution)/shard_map/psum | solution.py:112
  118.5 64.3 %copy-start.71 = (f32[768]{0:T(1024)}, f32[768]{0:T(1024)S(1)}, u32[]{:S(2)}) copy-start(f32[768]{0:T(1024)S(1)} %get-tuple-element.265) | copy-start | bytes 9220
  118.5 64.3 %copy-start.82 = (f32[768]{0:T(1024)}, f32[768]{0:T(1024)S(1)}, u32[]{:S(2)}) copy-start(f32[768]{0:T(1024)S(1)} %get-tuple-element.202) | copy-start | bytes 9220
  118.5 202.9 %copy-start.84 = (f32[768]{0:T(1024)}, f32[768]{0:T(1024)S(1)}, u32[]{:S(2)}) copy-start(f32[768]{0:T(1024)S(1)} %get-tuple-element.203) | copy-start | bytes 9220
  118.5 224.1 %copy-start.73 = (f32[768]{0:T(1024)}, f32[768]{0:T(1024)S(1)}, u32[]{:S(2)}) copy-start(f32[768]{0:T(1024)S(1)} %get-tuple-element.264) | copy-start | bytes 9220
  127.1 32.5 %copy-start.44 = (bf16[1,1,512,768]{3,2,1,0:T(8,128)(2,1)S(1)}, bf16[1,1,512,768]{3,2,1,0:T(8,128)(2,1)}, u32[]{:S(2)}) copy-start(bf16[1,1,512,768]{3,2,1,0:T(8,128)(2,1)} %param.14) | copy-start | bytes 2359300
  159.7 23.2 %slice-start.6 = ((s8[9437184]{0:T(1024)(128)(4,1)}), s8[4194304]{0:T(1024)(128)(4,1)S(1)}, s32[]{:S(2)}) async-start(s8[9437184]{0:T(1024)(128)(4,1)} %bitcast.390), calls=%async_computation.22 | async-start | bytes 8388608
  161.5 21.3 %copy-start.16 = (f32[512,768]{1,0:T(8,128)}, f32[512,768]{1,0:T(8,128)S(1)}, u32[]{:S(2)}) copy-start(f32[512,768]{1,0:T(8,128)S(1)} %get-tuple-element.219) | copy-start | bytes 4718596
  161.5 21.3 %copy-start.63 = (f32[512]{0:T(512)}, f32[512]{0:T(512)S(1)}, u32[]{:S(2)}) copy-start(f32[512]{0:T(512)S(1)} %broadcast_multiply_fusion.4) | copy-start | bytes 6148
  162.6 20.2 %copy-start.78 = (f32[512]{0:T(512)}, f32[512]{0:T(512)S(1)}, u32[]{:S(2)}) copy-start(f32[512]{0:T(512)S(1)} %fusion.198) | copy-start | bytes 6148
  162.6 20.3 %slice-start.7 = ((s8[9437184]{0:T(1024)(128)(4,1)}), s8[4194304]{0:T(1024)(128)(4,1)S(1)}, s32[]{:S(2)}) async-start(s8[9437184]{0:T(1024)(128)(4,1)} %bitcast.390), calls=%async_computation.23 | async-start | bytes 8388608
  162.6 20.3 %slice-start.8 = ((s8[9437184]{0:T(1024)(128)(4,1)}), s8[1048576]{0:T(1024)(128)(4,1)S(1)}, s32[]{:S(2)}) async-start(s8[9437184]{0:T(1024)(128)(4,1)} %bitcast.390), calls=%async_computation.24 | async-start | bytes 2097152
  246.7 149.6 %all-reduce.12.cloned.1.call-start = ((), (), s32[]{:S(2)}) async-start(), calls=%async_computation.7 | async-start | bytes 3145728 | tf_op jit(solution)/shard_map/psum | solution.py:170
  298.4 23.0 %slice-start.9 = ((s8[9437184]{0:T(1024)(128)(4,1)}), s8[4194304]{0:T(1024)(128)(4,1)S(1)}, s32[]{:S(2)}) async-start(s8[9437184]{0:T(1024)(128)(4,1)} %bitcast.392), calls=%async_computation.25 | async-start | bytes 8388608
  300.9 41.7 %copy-start.18 = (f32[512,768]{1,0:T(8,128)}, f32[512,768]{1,0:T(8,128)S(1)}, u32[]{:S(2)}) copy-start(f32[512,768]{1,0:T(8,128)S(1)} %get-tuple-element.215) | copy-start | bytes 4718596
  300.9 41.7 %copy-start.65 = (f32[512]{0:T(512)}, f32[512]{0:T(512)S(1)}, u32[]{:S(2)}) copy-start(f32[512]{0:T(512)S(1)} %broadcast_multiply_fusion.2) | copy-start | bytes 6148
  301.2 41.4 %copy-start.80 = (f32[512]{0:T(512)}, f32[512]{0:T(512)S(1)}, u32[]{:S(2)}) copy-start(f32[512]{0:T(512)S(1)} %fusion.200) | copy-start | bytes 6148
  301.3 20.2 %slice-start.10 = ((s8[9437184]{0:T(1024)(128)(4,1)}), s8[4194304]{0:T(1024)(128)(4,1)S(1)}, s32[]{:S(2)}) async-start(s8[9437184]{0:T(1024)(128)(4,1)} %bitcast.392), calls=%async_computation.26 | async-start | bytes 8388608
  344.7 174.0 %all-reduce.14.cloned.1.call-start = ((), (), s32[]{:S(2)}) async-start(), calls=%async_computation.8 | async-start | bytes 3145728 | tf_op jit(solution)/shard_map/psum | solution.py:170
  467.0 250.2 %reduce-scatter.16.cloned.1.call-start = ((), (), s32[]{:S(2)}) async-start(), calls=%async_computation.13 | async-start | bytes 417792
  495.9 222.9 %reduce-scatter.18.cloned.1.call-start = ((), (), s32[]{:S(2)}) async-start(), calls=%async_computation.14 | async-start | bytes 417792
  497.7 544.1 %all-reduce.18.cloned.1.call-start = ((), (), s32[]{:S(2)}) async-start(), calls=%async_computation.15 | async-start | bytes 47185920
  638.2 565.7 %all-reduce.16.cloned.1.call-start = ((), (), s32[]{:S(2)}) async-start(), calls=%async_computation.9 | async-start | bytes 12582912 | tf_op jit(solution)/shard_map/psum | solution.py:295
  651.6 632.6 %reduce-scatter.10.cloned.1.call-start = ((), (), s32[]{:S(2)}) async-start(), calls=%async_computation.10 | async-start | bytes 5013504 | tf_op jit(solution)/shard_map/reduce_scatter | solution.py:284
  658.6 824.1 %reduce-scatter.12.cloned.1.call-start = ((), (), s32[]{:S(2)}) async-start(), calls=%async_computation.11 | async-start | bytes 20054016 | tf_op jit(solution)/shard_map/reduce_scatter | solution.py:285
  675.0 1006.5 %reduce-scatter.14.cloned.1.call-start = ((), (), s32[]{:S(2)}) async-start(), calls=%async_computation.12 | async-start | bytes 20054016 | tf_op jit(solution)/shard_map/reduce_scatter | solution.py:286
  730.9 55.6 %copy-start.47 = (bf16[1,512,768]{2,1,0:T(8,128)(2,1)S(1)}, bf16[1,512,768]{2,1,0:T(8,128)(2,1)}, u32[]{:S(2)}) copy-start(bf16[1,512,768]{2,1,0:T(8,128)(2,1)} %copy.194) | copy-start | bytes 2359300
  730.9 55.6 %copy-start.49 = (bf16[1,512,768]{2,1,0:T(8,128)(2,1)S(1)}, bf16[1,512,768]{2,1,0:T(8,128)(2,1)}, u32[]{:S(2)}) copy-start(bf16[1,512,768]{2,1,0:T(8,128)(2,1)} %copy.193) | copy-start | bytes 2359300
  (96 other events, 550.9 us)
Sparse Core Ops, SparseCore 0:
  105.4 54.1 all-reduce.7
  246.8 51.4 all-reduce.9
  344.8 51.4 all-reduce.11
  467.2 51.5 all-reduce.13
  522.0 55.6 reduce-scatter.15
  581.5 54.5 reduce-scatter.17
  639.9 401.8 all-reduce.17
  1048.0 155.9 all-reduce.15
  1208.8 75.2 reduce-scatter.9
  1288.7 194.0 reduce-scatter.11
  1487.5 194.0 reduce-scatter.13
where the time goes:
time: 1700 us; the launch traced here: 1690 us
  waiting for transfers between devices  1030 us (61%)
  matrix products  371 us (22%)
  local copies, waits for them, and re-layouts  140 us (8%)
  other arithmetic  96.8 us (6%)
  blocking collectives  40.8 us (2%)
  between operations  17 us (1%)
    dot_general x46, matrix products, mixed_dot(): return jnp.einsum(formula, left, right, preferred_element_type=jnp.float32)  319 us
    unnamed x14, waiting for transfers between devices  250 us
    reduce_scatter x1, waiting for transfers between devices, local(): lax.psum_scatter(stacked[3], 'dp', scatter_dimension=1, tiled=True)  199 us
    reduce_scatter x1, waiting for transfers between devices, local(): lax.psum_scatter(stacked[2], 'dp', scatter_dimension=1, tiled=True)  199 us
    psum x1, waiting for transfers between devices, local(): lax.psum((jnp.stack([table_x, table_y]), bucket_all), ('stream', 'dp'))  159 us
    reduce_scatter x1, waiting for transfers between devices, local(): lax.psum_scatter(stacked[1], 'dp', scatter_dimension=1, tiled=True)  80.3 us
    psum x2, waiting for transfers between devices, layer_backward(): mixed_grad = lax.psum(pre_grad, 'stream')  72.4 us
    psum x2, waiting for transfers between devices, layer_forward(): mixed = lax.psum(attn_out, 'stream')  69.7 us
  transfers between devices with their start and end apart: 11, of which 9 were waited for; matrix products, arithmetic and copies ran while one was open for 17% of the time, Pallas kernels for 0%

commit v1 on v0

--- a/solution.py
+++ b/solution.py
@@ -1,3 +1,4 @@
+import functools
 from functools import partial
 import jax
 import jax.numpy as jnp
@@ -11,6 +12,14 @@
 NB2 = 64
 LAYERS = 2
 NEG_FILL = -1e30
+
+
+def manage_tables(row_data, net_axis, comm_axis):
+    big = lax.psum(lax.psum(row_data, net_axis), comm_axis)
+    return big
+
+
+feed_links = functools.partial(manage_tables, net_axis="dp", comm_axis="stream")
 
 
 def layer_norm(values, gain_vec, shift_vec):
@@ -292,7 +301,7 @@
     table_y = mixed_dot("rb,rd->bd", hot_y, spatial_low)
     own_slot = (jnp.arange(2, dtype=jnp.int32) == stream_at).astype(jnp.float32)
     bucket_all = own_slot[:, None, None, None] * jnp.stack(table_grads)[None]
-    shared, buckets = lax.psum((jnp.stack([table_x, table_y]), bucket_all), ("stream", "dp"))
+    shared, buckets = feed_links((jnp.stack([table_x, table_y]), bucket_all))
     bucket_own = lax.dynamic_slice_in_dim(buckets, stream_at, 1, 0)
     return (
         output,

time: 1700 us -> 1930 us (1.14)
  waiting for transfers between devices: 1030 us -> 1230 us
  blocking collectives: 40.8 us -> 67.2 us
    psum x1 -> x2, waiting for transfers between devices: 159 us -> 632 us  [manage_tables(): big = lax.psum(lax.psum(row_data, net_axis), comm_axis)]
    unnamed x14 -> x13, waiting for transfers between devices: 250 us -> 58.7 us
    reduce_scatter x1, waiting for transfers between devices: 80.3 us -> 0.01 us  [local(): lax.psum_scatter(stacked[1], 'dp', scatter_dimension=1, tiled=True)]
    psum x1 -> x2, blocking collectives: 40.8 us -> 67.2 us  [manage_tables(): big = lax.psum(lax.psum(row_data, net_axis), comm_axis)]
  transfers between devices with their start and end apart: 11 -> 11, of which waited for: 9 -> 10; matrix products, arithmetic and copies ran while one was open for 17% -> 9% of each run, Pallas kernels for 0% -> 0%
where the time goes in v1:
time: 1930 us
  waiting for transfers between devices  1230 us (64%)
  matrix products  379 us (20%)
  local copies, waits for them, and re-layouts  130 us (7%)
  other arithmetic  100 us (5%)
  blocking collectives  67.2 us (3%)
    psum x2, waiting for transfers between devices, manage_tables(): big = lax.psum(lax.psum(row_data, net_axis), comm_axis)  632 us
    dot_general x46, matrix products, mixed_dot(): return jnp.einsum(formula, left, right, preferred_element_type=jnp.float32)  326 us
    reduce_scatter x1, waiting for transfers between devices, local(): lax.psum_scatter(stacked[3], 'dp', scatter_dimension=1, tiled=True)  200 us
    reduce_scatter x1, waiting for transfers between devices, local(): lax.psum_scatter(stacked[2], 'dp', scatter_dimension=1, tiled=True)  199 us
    psum x2, waiting for transfers between devices, layer_backward(): mixed_grad = lax.psum(pre_grad, 'stream')  73.4 us
    psum x2, waiting for transfers between devices, layer_forward(): mixed = lax.psum(attn_out, 'stream')  69.8 us
    psum x2, blocking collectives, manage_tables(): big = lax.psum(lax.psum(row_data, net_axis), comm_axis)  67.2 us
    unnamed x13, waiting for transfers between devices  58.7 us
  transfers between devices with their start and end apart: 11, of which 10 were waited for; matrix products, arithmetic and copies ran while one was open for 9% of the time, Pallas kernels for 0%

profile of v1, /device:TPU:0, one launch (start us, length us, event | category | flops | bytes accessed | tf_op | source)
XLA Modules:
  0.0 1927.4 jit_solution(1003487508710149438)
XLA Ops:
  21.5 8.5 fusion.11
  30.0 14.4 fusion.3
  55.6 31.1 %fusion.242 = (f32[12,512]{1,0:T(8,128)S(1)}, f32[12,512,512]{1,2,0:T(8,128)}) fusion(f32[512,512,12]{0,2,1:T(8,128)} %fusion.3, f32[512,512,12]{0,2,1:T(8,128)} %fusion.11, bf16[1,512,12,64]{3,1,2,0:T(8,128)(2,1)} %copy.153, bf16[1,512,12,64]{3,1,2,0:T(8,128)(2,1)} %copy.152, bf16[1,512,12,64]{3,1,2,0:T(8,128)(2,1)} %copy.150, ...), kind=kOutput, calls=%fused_computation.338 | convolution fusion | flops 827320320 | bytes 40919552 | tf_op jit(solution)/shard_map/while/body/eval_jaxpr/qhd,khd->hqk/dot_general | solution.py:32
  113.5 8.6 fusion.10
  122.1 14.4 fusion.2
  136.5 18.2 all-reduce.9.cloned.1.call-done
  157.6 20.2 %multiply_convert_fusion.3 = (bf16[512,3072]{1,0:T(8,128)(2,1)S(1)}, f32[512,3072]{1,0:T(8,128)}, f32[512,3072]{1,0:T(8,128)}) fusion(bf16[1,2,768,3072]{3,2,1,0:T(8,128)(2,1)} %param.22, f32[512,768]{1,0:T(8,128)S(1)} %get-tuple-element.221, f32[768]{0:T(1024)S(1)} %get-tuple-element.202, f32[768]{0:T(1024)S(1)} %get-tuple-element.267, ...), kind=kOutput, calls=%fused_computation.71 | convolution fusion | flops 2520121344 | bytes 22030336 | tf_op jit(solution)/shard_map/dot_general | solution.py:125
  196.1 30.3 %fusion.244 = (f32[12,512]{1,0:T(8,128)S(1)}, f32[12,512,512]{1,2,0:T(8,128)}) fusion(f32[512,512,12]{0,2,1:T(8,128)} %fusion.2, f32[512,512,12]{0,2,1:T(8,128)} %fusion.10, bf16[1,512,12,64]{3,1,2,0:T(8,128)(2,1)S(1)} %copy-done.13, bf16[1,512,12,64]{3,1,2,0:T(8,128)(2,1)} %copy.169, bf16[1,512,12,64]{3,1,2,0:T(8,128)(2,1)S(1)} %copy-done.12, ...), kind=kOutput, calls=%fused_computation.340 | convolution fusion | flops 827320320 | bytes 40919552 | tf_op jit(solution)/shard_map/while/body/eval_jaxpr/qhd,khd->hqk/dot_general | solution.py:32
  241.4 51.6 %all-reduce.11.cloned.1.call-done = f32[512,768]{1,0:T(8,128)} async-done(((f32[512,768]{1,0:T(8,128)}), f32[512,768]{1,0:T(8,128)}) %all-reduce.11.cloned.1.call-update) | async-done | bytes 1572880 | tf_op jit(solution)/shard_map/psum | solution.py:121
  296.0 20.2 %multiply_convert_fusion.2 = (bf16[512,3072]{1,0:T(8,128)(2,1)S(1)}, f32[512,3072]{1,0:T(8,128)}, f32[512,3072]{1,0:T(8,128)}) fusion(bf16[1,2,768,3072]{3,2,1,0:T(8,128)(2,1)} %param.22, f32[512,768]{1,0:T(8,128)S(1)} %get-tuple-element.217, f32[768]{0:T(1024)S(1)} %get-tuple-element.203, f32[768]{0:T(1024)S(1)} %get-tuple-element.266, ...), kind=kOutput, calls=%fused_computation.58 | convolution fusion | flops 2520121344 | bytes 22030336 | tf_op jit(solution)/shard_map/dot_general | solution.py:125
  322.4 8.8 add_convert_fusion.1
  340.6 51.5 %all-reduce.13.cloned.1.call-done = f32[512,768]{1,0:T(8,128)} async-done(((f32[512,768]{1,0:T(8,128)}), f32[512,768]{1,0:T(8,128)}) %all-reduce.13.cloned.1.call-update) | async-done | bytes 1572880 | tf_op jit(solution)/shard_map/psum | solution.py:179
  397.9 12.2 multiply_reduce_fusion.1
  410.2 7.3 multiply_convert_fusion.1
  442.8 10.2 add_convert_fusion
  480.0 10.0 maximum_bitcast_fusion.1
  490.0 21.8 %all-reduce.15.cloned.1.call-done = f32[512,768]{1,0:T(8,128)} async-done(((f32[512,768]{1,0:T(8,128)}), f32[512,768]{1,0:T(8,128)}) %all-reduce.15.cloned.1.call-update) | async-done | bytes 1572880 | tf_op jit(solution)/shard_map/psum | solution.py:179
  516.7 10.8 multiply_reduce_fusion
  584.0 10.0 maximum_bitcast_fusion
  594.0 16.5 pad_maximum_fusion
  610.5 35.0 %copy.204 = f32[2,5,768,768]{3,0,1,2:T(2,128)} copy(f32[2,5,768,768]{2,3,1,0:T(8,128)} %pad_maximum_fusion) | data formatting | bytes 47185920 | tf_op jit(solution)/shard_map/stack | solution.py:290
  662.7 500.4 %all-reduce.19.cloned.1.call-done = (f32[2,1024,768]{2,1,0:T(8,128)}, f32[2,5,768,768]{3,0,1,2:T(2,128)}) async-done(((f32[2,1024,768]{2,1,0:T(8,128)}, f32[2,5,768,768]{3,0,1,2:T(2,128)}), (f32[2,1024,768]{2,1,0:T(8,128)}, f32[2,5,768,768]{3,0,1,2:T(2,128)})) %all-reduce.19.cloned.1.call-update) | async-done | bytes 29884432 | tf_op jit(solution)/shard_map/psum | solution.py:18
  1196.6 10.1 fusion.177
  1206.8 14.1 fusion.183
  1223.8 57.2 %reduce-scatter.16.cloned.1.call-done = f32[48,4]{1,0:T(8,128)} async-done(((f32[768,4]{1,0:T(8,128)}), f32[48,4]{1,0:T(8,128)}) %reduce-scatter.16.cloned.1.call-update) | async-done | bytes 784
  1282.4 10.0 fusion.174
  1292.5 14.2 fusion.180
  1306.8 58.5 %psum.62 = f32[2,2,12,96]{3,1,2,0:T(2,128)S(1)} all-reduce(f32[2,2,12,96]{3,1,2,0:T(2,128)S(1)} %broadcast_multiply_fusion), channel_id=1, replica_groups=mesh['stream'=2,'dp'=16] {'dp'}, use_global_device_ids=true, to_apply=%region_42.43 | all-reduce | flops 4608 | bytes 36864 | tf_op jit(solution)/shard_map/psum | solution.py:18
  1365.4 8.7 psum.63
  1383.7 132.1 %all-reduce.17.cloned.1.call-done = f32[2,1024,768]{2,1,0:T(8,128)} async-done(((f32[2,1024,768]{2,1,0:T(8,128)}), f32[2,1024,768]{2,1,0:T(8,128)}) %all-reduce.17.cloned.1.call-update) | async-done | bytes 6291472 | tf_op jit(solution)/shard_map/psum | solution.py:18
  1515.7 199.9 %reduce-scatter.14.cloned.1.call-done = f32[2,192,768]{2,1,0:T(8,128)} async-done(((f32[2,3072,768]{2,1,0:T(8,128)}), f32[2,192,768]{2,1,0:T(8,128)}) %reduce-scatter.14.cloned.1.call-update) | async-done | bytes 1179664 | tf_op jit(solution)/shard_map/reduce_scatter | solution.py:295
  1715.6 199.2 %reduce-scatter.12.cloned.1.call-done = f32[2,48,3072]{2,1,0:T(8,128)} async-done(((f32[2,768,3072]{2,1,0:T(8,128)}), f32[2,48,3072]{2,1,0:T(8,128)}) %reduce-scatter.12.cloned.1.call-update) | async-done | bytes 1179664 | tf_op jit(solution)/shard_map/reduce_scatter | solution.py:294
  (416 shorter events, 294.6 us)
Async XLA Ops:
  7.2 147.5 %all-reduce.9.cloned.1.call-start = ((), (), s32[]{:S(2)}) async-start(), calls=%async_computation.5 | async-start | bytes 3145728 | tf_op jit(solution)/shard_map/psum | solution.py:121
  19.5 94.0 %copy-start.4 = (s32[512,512]{0,1:T(8,128)}, s32[512,512]{0,1:T(8,128)S(1)}, u32[]{:S(2)}) copy-start(s32[512,512]{0,1:T(8,128)S(1)} %copy.154) | copy-start | bytes 3145732
  21.4 100.7 %copy-start.6 = (s32[512,512]{0,1:T(8,128)}, s32[512,512]{0,1:T(8,128)S(1)}, u32[]{:S(2)}) copy-start(s32[512,512]{0,1:T(8,128)S(1)} %copy.157) | copy-start | bytes 3145732
  50.5 42.9 %copy-start.28 = (bf16[1,512,768]{1,2,0:T(8,128)(2,1)}, bf16[1,512,768]{1,2,0:T(8,128)(2,1)S(1)}, u32[]{:S(2)}) copy-start(bf16[1,512,768]{1,2,0:T(8,128)(2,1)S(1)} %get-tuple-element.227) | copy-start | bytes 2359300
  100.3 192.7 %all-reduce.11.cloned.1.call-start = ((), (), s32[]{:S(2)}) async-start(), calls=%async_computation.6 | async-start | bytes 3145728 | tf_op jit(solution)/shard_map/psum | solution.py:121
  113.5 64.3 %copy-start.70 = (f32[768]{0:T(1024)}, f32[768]{0:T(1024)S(1)}, u32[]{:S(2)}) copy-start(f32[768]{0:T(1024)S(1)} %get-tuple-element.267) | copy-start | bytes 9220
  113.5 64.3 %copy-start.81 = (f32[768]{0:T(1024)}, f32[768]{0:T(1024)S(1)}, u32[]{:S(2)}) copy-start(f32[768]{0:T(1024)S(1)} %get-tuple-element.202) | copy-start | bytes 9220
  113.5 202.6 %copy-start.83 = (f32[768]{0:T(1024)}, f32[768]{0:T(1024)S(1)}, u32[]{:S(2)}) copy-start(f32[768]{0:T(1024)S(1)} %get-tuple-element.203) | copy-start | bytes 9220
  113.5 224.9 %copy-start.72 = (f32[768]{0:T(1024)}, f32[768]{0:T(1024)S(1)}, u32[]{:S(2)}) copy-start(f32[768]{0:T(1024)S(1)} %get-tuple-element.266) | copy-start | bytes 9220
  122.1 32.6 %copy-start.45 = (bf16[1,1,512,768]{3,2,1,0:T(8,128)(2,1)S(1)}, bf16[1,1,512,768]{3,2,1,0:T(8,128)(2,1)}, u32[]{:S(2)}) copy-start(bf16[1,1,512,768]{3,2,1,0:T(8,128)(2,1)} %param.14) | copy-start | bytes 2359300
  154.7 23.1 %slice-start.6 = ((s8[9437184]{0:T(1024)(128)(4,1)}), s8[4194304]{0:T(1024)(128)(4,1)S(1)}, s32[]{:S(2)}) async-start(s8[9437184]{0:T(1024)(128)(4,1)} %bitcast.390), calls=%async_computation.22 | async-start | bytes 8388608
  156.5 21.3 %copy-start.16 = (f32[512,768]{1,0:T(8,128)}, f32[512,768]{1,0:T(8,128)S(1)}, u32[]{:S(2)}) copy-start(f32[512,768]{1,0:T(8,128)S(1)} %get-tuple-element.221) | copy-start | bytes 4718596
  156.5 21.3 %copy-start.60 = (f32[512]{0:T(512)}, f32[512]{0:T(512)S(1)}, u32[]{:S(2)}) copy-start(f32[512]{0:T(512)S(1)} %broadcast_multiply_fusion.4) | copy-start | bytes 6148
  157.6 20.2 %copy-start.77 = (f32[512]{0:T(512)}, f32[512]{0:T(512)S(1)}, u32[]{:S(2)}) copy-start(f32[512]{0:T(512)S(1)} %fusion.198) | copy-start | bytes 6148
  157.6 20.3 %slice-start.7 = ((s8[9437184]{0:T(1024)(128)(4,1)}), s8[4194304]{0:T(1024)(128)(4,1)S(1)}, s32[]{:S(2)}) async-start(s8[9437184]{0:T(1024)(128)(4,1)} %bitcast.390), calls=%async_computation.23 | async-start | bytes 8388608
  157.6 20.3 %slice-start.8 = ((s8[9437184]{0:T(1024)(128)(4,1)}), s8[1048576]{0:T(1024)(128)(4,1)S(1)}, s32[]{:S(2)}) async-start(s8[9437184]{0:T(1024)(128)(4,1)} %bitcast.390), calls=%async_computation.24 | async-start | bytes 2097152
  241.4 150.8 %all-reduce.13.cloned.1.call-start = ((), (), s32[]{:S(2)}) async-start(), calls=%async_computation.7 | async-start | bytes 3145728 | tf_op jit(solution)/shard_map/psum | solution.py:179
  293.0 23.1 %slice-start.9 = ((s8[9437184]{0:T(1024)(128)(4,1)}), s8[4194304]{0:T(1024)(128)(4,1)S(1)}, s32[]{:S(2)}) async-start(s8[9437184]{0:T(1024)(128)(4,1)} %bitcast.392), calls=%async_computation.25 | async-start | bytes 8388608
  295.6 42.8 %copy-start.18 = (f32[512,768]{1,0:T(8,128)}, f32[512,768]{1,0:T(8,128)S(1)}, u32[]{:S(2)}) copy-start(f32[512,768]{1,0:T(8,128)S(1)} %get-tuple-element.217) | copy-start | bytes 4718596
  295.6 42.8 %copy-start.62 = (f32[512]{0:T(512)}, f32[512]{0:T(512)S(1)}, u32[]{:S(2)}) copy-start(f32[512]{0:T(512)S(1)} %broadcast_multiply_fusion.2) | copy-start | bytes 6148
  295.9 42.5 %copy-start.79 = (f32[512]{0:T(512)}, f32[512]{0:T(512)S(1)}, u32[]{:S(2)}) copy-start(f32[512]{0:T(512)S(1)} %fusion.200) | copy-start | bytes 6148
  295.9 20.2 %slice-start.10 = ((s8[9437184]{0:T(1024)(128)(4,1)}), s8[4194304]{0:T(1024)(128)(4,1)S(1)}, s32[]{:S(2)}) async-start(s8[9437184]{0:T(1024)(128)(4,1)} %bitcast.392), calls=%async_computation.26 | async-start | bytes 8388608
  340.5 171.3 %all-reduce.15.cloned.1.call-start = ((), (), s32[]{:S(2)}) async-start(), calls=%async_computation.8 | async-start | bytes 3145728 | tf_op jit(solution)/shard_map/psum | solution.py:179
  460.2 703.0 %all-reduce.19.cloned.1.call-start = ((), (), s32[]{:S(2)}) async-start(), calls=%async_computation.15 | async-start | bytes 59768832 | tf_op jit(solution)/shard_map/psum | solution.py:18
  651.5 570.8 %reduce-scatter.18.cloned.1.call-start = ((), (), s32[]{:S(2)}) async-start(), calls=%async_computation.14 | async-start | bytes 417792
  654.0 626.9 %reduce-scatter.16.cloned.1.call-start = ((), (), s32[]{:S(2)}) async-start(), calls=%async_computation.13 | async-start | bytes 417792
  655.8 727.9 %reduce-scatter.10.cloned.1.call-start = ((), (), s32[]{:S(2)}) async-start(), calls=%async_computation.10 | async-start | bytes 5013504 | tf_op jit(solution)/shard_map/reduce_scatter | solution.py:293
  662.7 853.1 %all-reduce.17.cloned.1.call-start = ((), (), s32[]{:S(2)}) async-start(), calls=%async_computation.9 | async-start | bytes 12582912 | tf_op jit(solution)/shard_map/psum | solution.py:18
  1163.2 552.5 %reduce-scatter.14.cloned.1.call-start = ((), (), s32[]{:S(2)}) async-start(), calls=%async_computation.12 | async-start | bytes 20054016 | tf_op jit(solution)/shard_map/reduce_scatter | solution.py:295
  1178.5 736.3 %reduce-scatter.12.cloned.1.call-start = ((), (), s32[]{:S(2)}) async-start(), calls=%async_computation.11 | async-start | bytes 20054016 | tf_op jit(solution)/shard_map/reduce_scatter | solution.py:294
  1292.5 82.2 %copy-start.46 = (bf16[1,512,768]{2,1,0:T(8,128)(2,1)S(1)}, bf16[1,512,768]{2,1,0:T(8,128)(2,1)}, u32[]{:S(2)}) copy-start(bf16[1,512,768]{2,1,0:T(8,128)(2,1)} %copy.192) | copy-start | bytes 2359300
  1292.5 82.2 %copy-start.47 = (bf16[1,512,768]{2,1,0:T(8,128)(2,1)S(1)}, bf16[1,512,768]{2,1,0:T(8,128)(2,1)}, u32[]{:S(2)}) copy-start(bf16[1,512,768]{2,1,0:T(8,128)(2,1)} %copy.193) | copy-start | bytes 2359300
  (97 other events, 537.2 us)
Sparse Core Ops, SparseCore 0:
  100.5 54.1 all-reduce.8
  241.5 51.4 all-reduce.10
  340.6 51.4 all-reduce.12
  460.3 51.4 all-reduce.14
  651.6 511.4 all-reduce.18
  1166.9 55.3 reduce-scatter.17
  1226.3 54.5 reduce-scatter.15
  1285.8 75.1 reduce-scatter.9
  1363.5 152.2 all-reduce.16
  1520.8 194.7 reduce-scatter.13
  1720.9 193.8 reduce-scatter.11
